TPU v7x, 256 devices: a whole 4x4x8 slice. The times are simulated.
256 devices in a mesh: row: 16 (over x, z_hi, core), loop: 16 (over y, z_lo).
Axes of the slice: x: 4, y: 4, z: 8 (z_hi: 2, z_lo: 4; z = z_hi * 4 + z_lo), core: 2. Of those that a mesh axis runs over, the one named last changes fastest.
Arguments:
- amplitudes: float32 [32768, 12288], P('row', 'loop'), may hold values from -6 to 6
- integrals: float32 [32768, 2048], P('row', 'loop'), may hold values from -0.046875 to 0.046875
- screen_mask: int32 [256, 16], P('row'), may hold values 0 or 1
- base_residual: float32 [2048, 12288], P('row', 'loop'), may hold values from -6 to 6
- vir_energy: float32 [2048], P('row'), may hold values from 0.5 to 4
- occ_energy: float32 [12288], P('loop'), may hold values from 0.5 to 2
Outputs:
- residual: float32 [2048, 12288], P('row', 'loop')
- update: float32 [2048, 12288], P('row', 'loop')
All inputs are finite; a program needn't handle non-finite values. No bound on the sum of `screen_mask` on one device may be relied on, other than what follows from the above.
Results may differ from a plain program's by a relative error of at most 0.000068.
Values sent between devices are 32-bit elements; how exact they have to be, the bound alone decides.
A program may use at most 128 MiB of HBM per device.

v0:
```python
import jax
import jax.numpy as jnp
from jax import lax
from jax.sharding import PartitionSpec as P

TILE = 128


def expand_mask(screen_mask, tile):
    rows_t, cols_t = screen_mask.shape
    values = screen_mask.astype(jnp.float32)
    return jnp.broadcast_to(values[:, None, :, None], (rows_t, tile, cols_t, tile)).reshape(
        rows_t * tile, cols_t * tile
    )


def contract(panel, amplitudes):
    return lax.dot_general(
        panel,
        amplitudes,
        (((0,), (0,)), ((), ())),
        precision=lax.Precision.HIGHEST,
        preferred_element_type=jnp.float32,
    )


def on_device(amplitudes, integrals, screen_mask, base_residual, vir_energy, occ_energy):
    full_mask = expand_mask(screen_mask, TILE)
    assembled = lax.all_gather(integrals, "loop", axis=1, tiled=True)
    screened = assembled * full_mask
    ladder = lax.psum_scatter(
        contract(screened, amplitudes), "row", scatter_dimension=0, tiled=True
    )
    residual = base_residual + ladder
    update = residual / (vir_energy[:, None] + occ_energy[None, :])
    return (residual, update)


def solution(mesh):
    in_specs = (
        P("row", "loop"),
        P("row", "loop"),
        P("row", None),
        P("row", "loop"),
        P("row"),
        P("loop"),
    )
    out_specs = (P("row", "loop"), P("row", "loop"))
    return jax.shard_map(
        on_device, mesh=mesh, in_specs=in_specs, out_specs=out_specs, check_vma=False
    )
```

profile of v0, /device:TPU:100, one launch (start us, length us, event | category | flops | bytes accessed | tf_op | source)
XLA Modules:
  0.0 544.5 jit_solution(3889775390057746643)
XLA Ops:
  7.2 0.0 all-gather.2.cloned.1.call-start
  7.2 0.7 all-gather.2.cloned.1.call-update
  7.9 0.0 reduce-scatter.2.cloned.1.call-start
  7.9 0.7 convert_element_type.3
  8.6 353.8 %all-gather.2.cloned.1.call-done = f32[2048,2048]{1,0:T(8,128)} async-done(((f32[2048,128]{1,0:T(8,128)}), f32[2048,2048]{1,0:T(8,128)}) %all-gather.2.cloned.1.call-update) | async-done | bytes 16777232 | tf_op jit(solution)/shard_map/all_gather | solution.py:29
  362.4 1.1 broadcast_in_dim.2
  363.6 0.0 copy-start
  363.6 0.0 copy-start.1
  363.6 0.0 copy-start.2
  363.6 54.1 %fusion = f32[2048,768]{1,0:T(8,128)} fusion(f32[2048,768]{1,0:T(8,128)} %param.6, f32[2048,2048]{1,0:T(8,128)} %all-gather.2.cloned.1.call-done, f32[256,8,16,128]{3,2,1,0:T(8,128)S(1)} %bitcast.6), kind=kOutput, calls=%fused_computation.1 | convolution fusion | flops 38658899968 | bytes 46137344 | tf_op jit(solution)/shard_map/dot_general | solution.py:18
  417.7 0.0 reduce-scatter.2.cloned.1.call-update
  417.7 118.0 %reduce-scatter.2.cloned.1.call-done = f32[128,768]{1,0:T(8,128)} async-done(((f32[2048,768]{1,0:T(8,128)}), f32[128,768]{1,0:T(8,128)}) %reduce-scatter.2.cloned.1.call-update) | async-done | bytes 393232 | tf_op jit(solution)/shard_map/reduce_scatter | solution.py:31
  535.7 0.0 copy-done
  535.7 0.0 copy-done.1
  535.7 0.0 copy-done.2
  535.7 1.9 add_divide_fusion
Async XLA Ops:
  7.2 355.3 %all-gather.2.cloned.1.call-start = ((), (), s32[]{:S(2)}) async-start(), calls=%async_computation.1 | async-start | bytes 17825792 | tf_op jit(solution)/shard_map/all_gather | solution.py:29
  7.9 527.8 %reduce-scatter.2.cloned.1.call-start = ((), (), s32[]{:S(2)}) async-start(), calls=%async_computation.2 | async-start | bytes 6684672 | tf_op jit(solution)/shard_map/reduce_scatter | solution.py:31
  363.6 172.1 %copy-start = (f32[128,768]{1,0:T(8,128)S(1)}, f32[128,768]{1,0:T(8,128)}, u32[]{:S(2)}) copy-start(f32[128,768]{1,0:T(8,128)} %param.9) | copy-start | bytes 1179652
  363.6 172.1 %copy-start.1 = (f32[768]{0:T(1024)S(1)}, f32[768]{0:T(1024)}, u32[]{:S(2)}) copy-start(f32[768]{0:T(1024)} %param.11) | copy-start | bytes 9220
  363.6 172.1 %copy-start.2 = (f32[128]{0:T(128)S(1)}, f32[128]{0:T(128)}, u32[]{:S(2)}) copy-start(f32[128]{0:T(128)} %param.10) | copy-start | bytes 1540
Sparse Core Ops, SparseCore 0:
  9.7 352.6 all-gather.1
  417.8 117.8 reduce-scatter.1
where the time goes:
time: 550 us; the launch traced here: 544 us
  waiting for transfers between devices  472 us (86%)
  matrix products  54.1 us (10%)
  between operations  14.1 us (3%)
    all_gather x1, waiting for transfers between devices, on_device(): assembled = lax.all_gather(integrals, 'loop', axis=1, tiled=True)  354 us
    reduce_scatter x1, waiting for transfers between devices, on_device(): lax.psum_scatter(contract(screened, amplitudes), 'row', scatter_dimension...  118 us
    dot_general x1, matrix products, contract(): lax.dot_general(panel, amplitudes, (((0,), (0,)), ((), ())), precision=la...  54.1 us
  transfers between devices with their start and end apart: 2, of which 2 were waited for; matrix products, arithmetic and copies ran while one was open for 0% of the time, Pallas kernels for 0%

commit v1 on v0

v1 whole, which is shorter than its diff:
```python
import jax
import jax.numpy as jnp
from jax import lax
from jax.experimental import pallas as pl
from jax.experimental.pallas import tpu as pltpu
from jax.sharding import PartitionSpec as P

TILE = 128
NL = 16
CR = 2048
HALF = CR // 2
IC = 768
BF = jnp.bfloat16
F32 = jnp.float32
MESH = pl.DeviceIdType.MESH


def kernel(
    amp_hbm,
    int_hbm,
    mask,
    out,
    blk,
    t32,
    tth,
    ttl,
    rhs,
    pbuf,
    crecv,
    xrecv,
    zrecv,
    load_sem,
    g_recv,
    y_send,
    yf_send,
    z_send,
    zf_send,
    c_send,
    c_recv,
    x_send,
    x_recv,
    h_send,
    h_recv,
):
    row = lax.axis_index("row")
    loop = lax.axis_index("loop")
    x, zh, core = row // 4, (row // 2) % 2, row % 2
    y, z = loop // 4, loop % 4
    zq = z // 2
    inner = ((z + 1) // 2) % 2 == 1
    ys = [y, (y + 1) % 4, (y + 3) % 4, (y + 2) % 4]
    zs = [z, z + 1 - 2 * (z % 2), 2 - zq, 3 - 3 * zq]

    def slot(d, k):
        return ys[d] * 4 + zs[k]

    up = (row, ys[1] * 4 + z)
    down = (row, ys[2] * 4 + z)
    znear = (row, y * 4 + zs[1])
    zfar = (row, y * 4 + 3 - z)
    mate = (row + 1 - 2 * core, loop)
    hpeer = (row + 2 - 4 * zh, loop)

    barrier = pltpu.get_barrier_semaphore()
    peers = [up, down, znear, mate, hpeer]
    peers += [(((x + j) % 4) * 4 + zh * 2 + core, loop) for j in (1, 2, 3)]
    for peer in peers:
        pl.semaphore_signal(barrier, inc=1, device_id=peer, device_id_type=MESH)

    @pl.when(inner)
    def _():
        pl.semaphore_signal(barrier, inc=1, device_id=zfar, device_id_type=MESH)

    load_t = pltpu.make_async_copy(amp_hbm, t32, load_sem.at[0])
    load_t.start()
    load_b = pltpu.make_async_copy(int_hbm, blk.at[loop], load_sem.at[1])
    load_b.start()
    pl.semaphore_wait(barrier, len(peers) + ((z + 1) // 2) % 2)

    def remote(src, dst, send, recv, to):
        return pltpu.make_async_remote_copy(
            src_ref=src,
            dst_ref=dst,
            send_sem=send,
            recv_sem=recv,
            device_id=to,
            device_id_type=MESH,
        )

    def g_copy(s, h, send, to, own=False):
        src = int_hbm.at[h] if own else blk.at[s, h]
        return remote(src, blk.at[s, h], send, g_recv.at[s, h], to)

    def arrived(d, k, h):
        s = slot(d, k)
        g_copy(s, h, y_send.at[0, 0, 0], up).wait_recv()

    def y_copies(k):
        s = slot(0, k)
        own = k == 0
        return [
            g_copy(s, 0, y_send.at[0, k, 0], up, own),
            g_copy(s, 1, y_send.at[1, k, 1], down, own),
            g_copy(s, 1, y_send.at[0, k, 1], up, own),
            g_copy(s, 0, y_send.at[1, k, 0], down, own),
        ]

    def zf_copies(k):
        s = slot(0, k)
        to = znear if k > 1 else zfar
        return [g_copy(s, h, zf_send.at[k - 1, h], to) for h in (0, 1)]

    def z_copies(far):
        to = zfar if far else znear
        return [g_copy(loop, h, z_send.at[far, h], to, True) for h in (0, 1)]

    def f_copies(k):
        return [
            g_copy(slot(2, k), 0, yf_send.at[0, k], up),
            g_copy(slot(1, k), 1, yf_send.at[1, k], down),
        ]

    for c in z_copies(0):
        c.start()

    @pl.when(inner)
    def _():
        for c in z_copies(1):
            c.start()

    for c in y_copies(0):
        c.start()

    load_t.wait()

    def prep(j, carry):
        at = pl.multiple_of(j * 128, 128)
        t = t32[pl.ds(at, 128), :].T
        hi = t.astype(BF)
        tth[:, pl.ds(at, 128)] = hi
        ttl[:, pl.ds(at, 128)] = (t - hi.astype(F32)).astype(BF)
        return carry

    lax.fori_loop(0, CR // 128, prep, 0)

    def compute(d, k):
        s = slot(d, k)

        def split(j, carry):
            h, at = j // 8, pl.multiple_of((j % 8) * 128, 128)
            m = blk[s, h, pl.ds(at, 128), :] * mask[j, s].astype(F32)
            hi = m.astype(BF)
            lo = (m - hi.astype(F32)).astype(BF)
            to = pl.multiple_of(j * 128, 128)
            rhs[pl.ds(to, 128), 0:128] = hi
            rhs[pl.ds(to, 128), 128:256] = lo
            return carry

        lax.fori_loop(0, 16, split, 0)

        def rows(j, carry):
            at = pl.multiple_of(j * 256, 256)
            a = jnp.dot(tth[pl.ds(at, 256), :], rhs[...], preferred_element_type=F32)
            b = jnp.dot(ttl[pl.ds(at, 256), :], rhs[:, 0:128], preferred_element_type=F32)
            pbuf[s, pl.ds(at, 256), :] = a[:, 0:128] + (a[:, 128:256] + b)
            return carry

        lax.fori_loop(0, IC // 256, rows, 0)

        @pl.when((zs[k] + core) % 2 == 1)
        def _():
            c_copy(d, k // 2, s).start()

    def c_copy(d, p, s):
        n = d * 2 + p
        return remote(pbuf.at[s], crecv.at[n], c_send.at[n], c_recv.at[n], mate)

    def keep_slot(yv, p):
        return yv * 4 + 2 * ((zq + p) % 2) + core

    def x_copy(d, p):
        yv = ys[d]
        s = keep_slot(yv, p)
        place = (x + 4 - yv) % 4 - 1
        to = (yv * 4 + zh * 2 + core, loop)
        return remote(
            pbuf.at[s], xrecv.at[place, p], x_send.at[d, p], x_recv.at[place, p], to
        )

    def reduce_pair(d, p):
        n = d * 2 + p
        s = keep_slot(ys[d], p)
        c_copy(d, p, s).wait_recv()
        pbuf[s] = pbuf[s] + crecv[n]

        @pl.when(x != ys[d])
        def _():
            x_copy(d, p).start()

    def y_out(k):
        for c in y_copies(k):
            c.start()

    def z_forward(k):
        for h in (0, 1):
            arrived(0, k, h)

        @pl.when(inner)
        def _():
            for c in zf_copies(k):
                c.start()

    def y_forward(k):
        arrived(2, k, 0)
        up_c, down_c = f_copies(k)
        up_c.start()
        arrived(1, k, 1)
        down_c.start()

    def rest(k):
        arrived(1, k, 0)
        arrived(2, k, 1)

    def last(k):
        arrived(3, k, 0)
        arrived(3, k, 1)

    load_b.wait()
    compute(0, 0)
    z_forward(1)
    y_out(1)
    y_forward(0)
    rest(0)
    compute(0, 1)
    compute(1, 0)
    compute(2, 0)
    reduce_pair(0, 0)
    z_forward(2)
    y_out(2)
    y_forward(1)
    rest(1)
    compute(0, 2)
    compute(1, 1)
    compute(2, 1)
    reduce_pair(1, 0)
    last(0)
    compute(3, 0)
    reduce_pair(2, 0)
    z_forward(3)
    y_out(3)
    compute(0, 3)
    y_forward(2)
    rest(2)
    compute(1, 2)
    reduce_pair(0, 1)
    compute(2, 2)
    last(1)
    compute(3, 1)
    y_forward(3)
    reduce_pair(3, 0)
    rest(3)
    compute(1, 3)
    compute(2, 3)
    reduce_pair(1, 1)
    last(2)
    compute(3, 2)
    reduce_pair(2, 1)
    last(3)
    compute(3, 3)
    reduce_pair(3, 1)

    def x_total(p):
        s = keep_slot(x, p)
        for j in range(3):
            remote(
                pbuf.at[s], xrecv.at[j, p], x_send.at[0, 0], x_recv.at[j, p], mate
            ).wait_recv()
        pbuf[s] = pbuf[s] + ((xrecv[0, p] + xrecv[1, p]) + xrecv[2, p])
        return s

    p_mine = (zq + zh) % 2
    p_send = 1 - p_mine
    s_send = x_total(p_send)
    h_copy = remote(pbuf.at[s_send], zrecv, h_send, h_recv, hpeer)
    h_copy.start()
    s_mine = x_total(p_mine)
    h_copy.wait_recv()
    out[...] = (pbuf[s_mine] + zrecv[...]).T

    h_copy.wait_send()
    for c in z_copies(0):
        c.wait_send()
    for k in range(4):
        for c in y_copies(k):
            c.wait_send()
        for c in f_copies(k):
            c.wait_send()

    @pl.when(inner)
    def _():
        for c in z_copies(1):
            c.wait_send()
        for k in (1, 2, 3):
            for c in zf_copies(k):
                c.wait_send()

    for d in range(4):
        for p in range(2):
            c_copy(d, p, loop).wait_send()

        @pl.when(x != ys[d])
        def _():
            for p in range(2):
                x_copy(d, p).wait_send()


def ladder_of(amplitudes, integrals, screen_mask):
    dma = pltpu.SemaphoreType.DMA
    return pl.pallas_call(
        kernel,
        out_shape=jax.ShapeDtypeStruct((TILE, IC), F32),
        in_specs=[
            pl.BlockSpec(memory_space=pl.ANY),
            pl.BlockSpec(memory_space=pl.ANY),
            pl.BlockSpec(memory_space=pltpu.SMEM),
        ],
        out_specs=pl.BlockSpec(memory_space=pltpu.VMEM),
        scratch_shapes=[
            pltpu.VMEM((NL, 2, HALF, TILE), F32),
            pltpu.VMEM((CR, IC), F32),
            pltpu.VMEM((IC, CR), BF),
            pltpu.VMEM((IC, CR), BF),
            pltpu.VMEM((CR, 2 * TILE), BF),
            pltpu.VMEM((NL, IC, TILE), F32),
            pltpu.VMEM((8, IC, TILE), F32),
            pltpu.VMEM((3, 2, IC, TILE), F32),
            pltpu.VMEM((IC, TILE), F32),
            dma((2,)),
            dma((NL, 2)),
            dma((2, 4, 2)),
            dma((2, 4)),
            dma((2, 2)),
            dma((3, 2)),
            dma((8,)),
            dma((8,)),
            dma((4, 2)),
            dma((3, 2)),
            dma,
            dma,
        ],
        compiler_params=pltpu.CompilerParams(
            collective_id=0, has_side_effects=True, vmem_limit_bytes=60 * 1024 * 1024
        ),
        cost_estimate=pl.CostEstimate(
            flops=2 * 3 * CR * CR * IC, bytes_accessed=24 * 2**20, transcendentals=0
        ),
    )(amplitudes, integrals.reshape(2, HALF, TILE), screen_mask)


def on_device(amplitudes, integrals, screen_mask, base_residual, vir_energy, occ_energy):
    ladder = ladder_of(amplitudes, integrals, screen_mask)
    residual = base_residual + ladder
    update = residual / (vir_energy[:, None] + occ_energy[None, :])
    return (residual, update)


def solution(mesh):
    in_specs = (
        P("row", "loop"),
        P("row", "loop"),
        P("row", None),
        P("row", "loop"),
        P("row"),
        P("loop"),
    )
    out_specs = (P("row", "loop"), P("row", "loop"))
    return jax.shard_map(
        on_device, mesh=mesh, in_specs=in_specs, out_specs=out_specs, check_vma=False
    )
```

time: 550 us -> 190 us (0.35)
  waiting for transfers between devices: 472 us -> 0 us
  Pallas kernels: 0 us -> 185 us
  matrix products: 54.1 us -> 0 us
  between operations: 14.1 us -> 0.69 us
    all_gather x1 -> x0, waiting for transfers between devices: 354 us -> none  [on_device(): assembled = lax.all_gather(integrals, 'loop', axis=1, tiled=True)]
    pallas_call x0 -> x1, Pallas kernels: none -> 185 us  [ladder_of(): pl.pallas_call(kernel, out_shape=jax.ShapeDtypeStruct((TILE, IC), F32), i...]
    reduce_scatter x1 -> x0, waiting for transfers between devices: 118 us -> none  [on_device(): lax.psum_scatter(contract(screened, amplitudes), 'row', scatter_dimension...]
    dot_general x1 -> x0, matrix products: 54.1 us -> none  [contract(): lax.dot_general(panel, amplitudes, (((0,), (0,)), ((), ())), precision=la...]
  transfers between devices with their start and end apart: 2 -> 0, of which waited for: 2 -> 0; matrix products, arithmetic and copies ran while one was open for 0% -> 0% of each run, Pallas kernels for 0% -> 0%
where the time goes in v1:
time: 190 us; the launch traced here: 187 us
  Pallas kernels  185 us (97%)
  other arithmetic  1.92 us (1%)
    pallas_call x1, Pallas kernels, ladder_of(): pl.pallas_call(kernel, out_shape=jax.ShapeDtypeStruct((TILE, IC), F32), i...  185 us

profile of v1, /device:TPU:100, one launch (start us, length us, event | category | flops | bytes accessed | tf_op | source)
XLA Modules:
  0.0 187.4 jit_solution(15264058666033434591)
XLA Ops:
  0.6 0.0 copy-start
  0.6 0.0 copy-start.1
  0.7 0.0 copy-start.2
  0.7 184.8 %shard_map.77 = f32[128,768]{1,0:T(8,128)} custom-call(f32[2048,768]{1,0:T(8,128)} %amp_hbm.1, f32[2,1024,128]{2,1,0:T(8,128)} %bitcast.1, s32[16,16]{1,0:T(8,128)} %mask.1), custom_call_target="tpu_custom_call" | custom-call | flops 19327352832 | bytes 25165824 | tf_op jit(solution)/shard_map/pallas_call | solution.py:319
  185.5 0.0 copy-done
  185.5 0.0 copy-done.1
  185.5 0.0 copy-done.2
  185.5 1.9 %add_divide_fusion = (f32[128,768]{1,0:T(8,128)}, f32[128,768]{1,0:T(8,128)}) fusion(f32[768]{0:T(1024)S(1)} %copy-done.1, f32[128]{0:T(128)S(1)} %copy-done.2, f32[128,768]{1,0:T(8,128)S(1)} %copy-done, f32[128,768]{1,0:T(8,128)} %shard_map.77), kind=kLoop, calls=%fused_computation | loop fusion | flops 294912 | bytes 1576448 | tf_op jit(solution)/shard_map/div | solution.py:363
Async XLA Ops:
  0.6 184.8 %copy-start = (f32[128,768]{1,0:T(8,128)S(1)}, f32[128,768]{1,0:T(8,128)}, u32[]{:S(2)}) copy-start(f32[128,768]{1,0:T(8,128)} %param.9) | copy-start | bytes 1179652
  0.6 184.8 %copy-start.1 = (f32[768]{0:T(1024)S(1)}, f32[768]{0:T(1024)}, u32[]{:S(2)}) copy-start(f32[768]{0:T(1024)} %param.11) | copy-start | bytes 9220
  0.7 184.8 %copy-start.2 = (f32[128]{0:T(128)S(1)}, f32[128]{0:T(128)}, u32[]{:S(2)}) copy-start(f32[128]{0:T(128)} %param.10) | copy-start | bytes 1540

commit v2 on v1

v2 whole, which is shorter than its diff:
```python
import jax
import jax.numpy as jnp
from jax import lax
from jax.experimental import pallas as pl
from jax.experimental.pallas import tpu as pltpu
from jax.sharding import PartitionSpec as P

TILE = 128
NL = 16
CR = 2048
FIRST_Y = 336
NA = (CR - FIRST_Y) // 2
NB = FIRST_Y // 2
A0, A1, B0, B1, BB = (0, NA), (NA, NA), (2 * NA, NB), (2 * NA + NB, NB), (2 * NA, FIRST_Y)
SEM = {A0: 0, A1: 1, B0: 2, B1: 3, BB: 2}
TI = 256
NT = 3
IC = 768
BF = jnp.bfloat16
F32 = jnp.float32
MESH = pl.DeviceIdType.MESH


def kernel(
    amp_hbm,
    int_hbm,
    mask,
    out,
    blk,
    t32,
    tth,
    ttl,
    rhs,
    pbuf,
    crecv,
    xrecv,
    zrecv,
    load_sem,
    g_recv,
    y_send,
    yb_send,
    yf_send,
    z_send,
    zf_send,
    zb_send,
    zbf_send,
    c_send,
    c_recv,
    x_send,
    x_recv,
    h_send,
    h_recv,
):
    row = lax.axis_index("row")
    loop = lax.axis_index("loop")
    x, zh, core = row // 4, (row // 2) % 2, row % 2
    y, z = loop // 4, loop % 4
    zq = z // 2
    inner = ((z + 1) // 2) % 2 == 1
    ys = [y, (y + 1) % 4, (y + 3) % 4, (y + 2) % 4]
    zs = [z, z + 1 - 2 * (z % 2), 2 - zq, 3 - 3 * zq]

    def slot(d, k):
        return ys[d] * 4 + zs[k]

    up = (row, ys[1] * 4 + z)
    down = (row, ys[2] * 4 + z)
    znear = (row, y * 4 + zs[1])
    zfar = (row, y * 4 + 3 - z)
    mate = (row + 1 - 2 * core, loop)
    hpeer = (row + 2 - 4 * zh, loop)

    barrier = pltpu.get_barrier_semaphore()
    peers = [up, down, znear, mate, hpeer]
    peers += [(((x + j) % 4) * 4 + zh * 2 + core, loop) for j in (1, 2, 3)]
    for peer in peers:
        pl.semaphore_signal(barrier, inc=1, device_id=peer, device_id_type=MESH)

    @pl.when(inner)
    def _():
        pl.semaphore_signal(barrier, inc=1, device_id=zfar, device_id_type=MESH)

    load_t = pltpu.make_async_copy(amp_hbm, t32, load_sem.at[0])
    load_t.start()
    load_b = pltpu.make_async_copy(int_hbm, blk.at[loop], load_sem.at[1])
    load_b.start()
    pl.semaphore_wait(barrier, len(peers) + ((z + 1) // 2) % 2)

    def remote(src, dst, send, recv, to):
        return pltpu.make_async_remote_copy(
            src_ref=src,
            dst_ref=dst,
            send_sem=send,
            recv_sem=recv,
            device_id=to,
            device_id_type=MESH,
        )

    def g_copy(s, part, send, to, own=False):
        view = pl.ds(part[0], part[1])
        src = int_hbm.at[view] if own else blk.at[s, view]
        return remote(src, blk.at[s, view], send, g_recv.at[s, SEM[part]], to)

    def arrived(d, k, part):
        g_copy(slot(d, k), part, y_send.at[0, 0, 0], up).wait_recv()

    def y_copies(k):
        s = slot(0, k)
        own = k == 0
        return [
            g_copy(s, A0, y_send.at[0, k, 0], up, own),
            g_copy(s, A1, y_send.at[1, k, 1], down, own),
            g_copy(s, A1, y_send.at[0, k, 1], up, own),
            g_copy(s, A0, y_send.at[1, k, 0], down, own),
        ]

    def yb_copies():
        return [g_copy(loop, BB, yb_send.at[n], to, True) for n, to in enumerate((up, down))]

    def zf_copies(k):
        s = slot(0, k)
        to = znear if k > 1 else zfar
        return [g_copy(s, h, zf_send.at[k - 1, n], to) for n, h in enumerate((A0, A1))]

    def z_copies(far):
        to = zfar if far else znear
        return [g_copy(loop, h, z_send.at[far, n], to, True) for n, h in enumerate((A0, A1))]

    def zb_copies(far):
        to = zfar if far else znear
        return [g_copy(slot(d, 0), BB, zb_send.at[far, d], to) for d in range(4)]

    def zbf_copies(k):
        to = znear if k > 1 else zfar
        return [g_copy(slot(d, k), BB, zbf_send.at[k - 1, d], to) for d in range(4)]

    def f_copies(k):
        return [
            g_copy(slot(2, k), A0, yf_send.at[0, k], up),
            g_copy(slot(1, k), A1, yf_send.at[1, k], down),
        ]

    def fb_copies():
        return [
            g_copy(slot(2, 0), B0, yf_send.at[0, 4], up),
            g_copy(slot(1, 0), B1, yf_send.at[1, 4], down),
        ]

    for c in z_copies(0):
        c.start()

    @pl.when(inner)
    def _():
        for c in z_copies(1):
            c.start()

    for c in yb_copies() + y_copies(0):
        c.start()

    load_t.wait()

    def prep(j, carry):
        at = pl.multiple_of(j * 128, 128)
        t = t32[pl.ds(at, 128), :].T
        hi = t.astype(BF)
        tth[:, pl.ds(at, 128)] = hi
        ttl[:, pl.ds(at, 128)] = (t - hi.astype(F32)).astype(BF)
        return carry

    lax.fori_loop(0, CR // 128, prep, 0)

    def split(s):
        def body(j, carry):
            at = pl.multiple_of(j * 128, 128)
            m = blk[s, pl.ds(at, 128), :] * mask[j, s].astype(F32)
            hi = m.astype(BF)
            rhs[pl.ds(at, 128), 0:128] = hi
            rhs[pl.ds(at, 128), 128:256] = (m - hi.astype(F32)).astype(BF)
            return carry

        lax.fori_loop(0, CR // 128, body, 0)

    def multiply(s, j):
        at = pl.ds(pl.multiple_of(j * TI, TI), TI)
        a = jnp.dot(tth[at, :], rhs[...], preferred_element_type=F32)
        b = jnp.dot(ttl[at, :], rhs[:, 0:128], preferred_element_type=F32)
        pbuf[s, at, :] = a[:, 0:128] + (a[:, 128:256] + b)

    def tile(j):
        return pl.ds(j * TI, TI)

    def c_copy(d, k, j):
        n = d * 2 + k // 2
        return remote(
            pbuf.at[slot(d, k), tile(j)],
            crecv.at[n, tile(j)],
            c_send.at[n, j],
            c_recv.at[n, j],
            mate,
        )

    def keeps(k):
        return (zs[k] + core) % 2 == 0

    def x_copy(d, p, s, j):
        yv = ys[d]
        place = (x + 4 - yv) % 4 - 1
        to = (yv * 4 + zh * 2 + core, loop)
        return remote(
            pbuf.at[s, tile(j)],
            xrecv.at[place, p, tile(j)],
            x_send.at[d, p, j],
            x_recv.at[place, p, j],
            to,
        )

    def to_mate(d, k, j):
        @pl.when(jnp.logical_not(keeps(k)))
        def _():
            c_copy(d, k, j).start()

    def reduce(d, k, j):
        @pl.when(keeps(k))
        def _():
            n = d * 2 + k // 2
            s = slot(d, k)
            c_copy(d, k, j).wait_recv()
            pbuf[s, tile(j)] = pbuf[s, tile(j)] + crecv[n, tile(j)]

            @pl.when(x != ys[d])
            def _():
                x_copy(d, k // 2, s, j).start()

    def compute(d, k):
        s = slot(d, k)
        split(s)

        def body(j, carry):
            multiply(s, j)
            return carry

        lax.fori_loop(0, NT, body, 0)
        for j in range(NT):
            to_mate(d, k, j)

    def reduce_all(d, k):
        for j in range(NT):
            reduce(d, k, j)

    def y_out(k):
        for c in y_copies(k):
            c.start()

    def z_forward(k):
        for part in (A0, A1):
            arrived(0, k, part)

        @pl.when(inner)
        def _():
            for c in zf_copies(k):
                c.start()

    def zb_forward(k):
        for d in range(4):
            arrived(d, k, BB)

        @pl.when(inner)
        def _():
            for c in zbf_copies(k):
                c.start()

    def y_forward(k):
        up_c, down_c = f_copies(k)
        arrived(2, k, A0)
        up_c.start()
        arrived(1, k, A1)
        down_c.start()

    def rest(k):
        arrived(1, k, A0)
        arrived(2, k, A1)

    def last(k):
        arrived(3, k, A0)
        arrived(3, k, A1)

    def x_total(p):
        s = x * 4 + 2 * ((zq + p) % 2) + core
        for j in range(NT):
            for i in range(3):
                remote(
                    pbuf.at[s, tile(j)],
                    xrecv.at[i, p, tile(j)],
                    x_send.at[0, 0, 0],
                    x_recv.at[i, p, j],
                    mate,
                ).wait_recv()
            pbuf[s, tile(j)] = pbuf[s, tile(j)] + (
                (xrecv[0, p, tile(j)] + xrecv[1, p, tile(j)]) + xrecv[2, p, tile(j)]
            )

            @pl.when((zq + zh + p) % 2 == 1)
            def _():
                h_copy(s, j).start()

    def h_copy(s, j):
        return remote(
            pbuf.at[s, tile(j)], zrecv.at[tile(j)], h_send.at[j], h_recv.at[j], hpeer
        )

    up_b, down_b = fb_copies()
    arrived(2, 0, BB)
    up_b.start()
    arrived(1, 0, BB)
    down_b.start()
    load_b.wait()
    compute(0, 0)
    z_forward(1)
    y_out(1)
    arrived(3, 0, B0)
    arrived(3, 0, B1)
    for c in zb_copies(0):
        c.start()

    @pl.when(inner)
    def _():
        for c in zb_copies(1):
            c.start()

    y_forward(0)
    rest(0)
    compute(1, 0)
    compute(2, 0)
    z_forward(2)
    y_out(2)
    y_forward(1)
    rest(1)
    last(0)
    compute(3, 0)
    zb_forward(1)
    compute(0, 1)
    reduce_all(0, 0)
    reduce_all(0, 1)
    z_forward(3)
    y_out(3)
    compute(1, 1)
    reduce_all(1, 0)
    reduce_all(1, 1)
    compute(2, 1)
    reduce_all(2, 0)
    reduce_all(2, 1)
    y_forward(2)
    rest(2)
    zb_forward(2)
    compute(0, 2)
    compute(1, 2)
    last(1)
    compute(3, 1)
    reduce_all(3, 0)
    reduce_all(3, 1)
    compute(2, 2)
    zb_forward(3)
    y_forward(3)
    rest(3)
    compute(0, 3)
    reduce_all(0, 2)
    reduce_all(0, 3)
    compute(1, 3)
    reduce_all(1, 2)
    reduce_all(1, 3)
    compute(2, 3)
    reduce_all(2, 2)
    reduce_all(2, 3)
    x_total(0)
    last(2)
    compute(3, 2)
    reduce_all(3, 2)
    last(3)
    s_last = slot(3, 3)
    split(s_last)
    multiply(s_last, 0)
    to_mate(3, 3, 0)
    multiply(s_last, 1)
    to_mate(3, 3, 1)
    reduce(3, 3, 0)
    multiply(s_last, 2)
    to_mate(3, 3, 2)
    reduce(3, 3, 1)
    reduce(3, 3, 2)
    x_total(1)
    s_mine = x * 4 + 2 * zh + core
    for j in range(NT):
        h_copy(s_mine, j).wait_recv()
        out[:, j * TI : (j + 1) * TI] = (pbuf[s_mine, tile(j)] + zrecv[tile(j)]).T

    for j in range(NT):
        h_copy(s_mine, j).wait_send()
    for c in z_copies(0) + yb_copies() + fb_copies() + zb_copies(0):
        c.wait_send()
    for k in range(4):
        for c in y_copies(k) + f_copies(k):
            c.wait_send()

    @pl.when(inner)
    def _():
        for c in z_copies(1) + zb_copies(1):
            c.wait_send()
        for k in (1, 2, 3):
            for c in zf_copies(k) + zbf_copies(k):
                c.wait_send()

    for d in range(4):
        for p in range(2):
            for j in range(NT):
                c_copy(d, 2 * p, j).wait_send()

        @pl.when(x != ys[d])
        def _():
            for p in range(2):
                for j in range(NT):
                    x_copy(d, p, loop, j).wait_send()


def ladder_of(amplitudes, integrals, screen_mask):
    dma = pltpu.SemaphoreType.DMA
    return pl.pallas_call(
        kernel,
        out_shape=jax.ShapeDtypeStruct((TILE, IC), F32),
        in_specs=[
            pl.BlockSpec(memory_space=pl.ANY),
            pl.BlockSpec(memory_space=pl.ANY),
            pl.BlockSpec(memory_space=pltpu.SMEM),
        ],
        out_specs=pl.BlockSpec(memory_space=pltpu.VMEM),
        scratch_shapes=[
            pltpu.VMEM((NL, CR, TILE), F32),
            pltpu.VMEM((CR, IC), F32),
            pltpu.VMEM((IC, CR), BF),
            pltpu.VMEM((IC, CR), BF),
            pltpu.VMEM((CR, 2 * TILE), BF),
            pltpu.VMEM((NL, IC, TILE), F32),
            pltpu.VMEM((8, IC, TILE), F32),
            pltpu.VMEM((3, 2, IC, TILE), F32),
            pltpu.VMEM((IC, TILE), F32),
            dma((2,)),
            dma((NL, 4)),
            dma((2, 4, 2)),
            dma((2,)),
            dma((2, 5)),
            dma((2, 2)),
            dma((3, 2)),
            dma((2, 4)),
            dma((3, 4)),
            dma((8, NT)),
            dma((8, NT)),
            dma((4, 2, NT)),
            dma((3, 2, NT)),
            dma((NT,)),
            dma((NT,)),
        ],
        compiler_params=pltpu.CompilerParams(
            collective_id=0, has_side_effects=True, vmem_limit_bytes=60 * 1024 * 1024
        ),
        cost_estimate=pl.CostEstimate(
            flops=2 * 3 * CR * CR * IC, bytes_accessed=24 * 2**20, transcendentals=0
        ),
    )(amplitudes, integrals, screen_mask)


def on_device(amplitudes, integrals, screen_mask, base_residual, vir_energy, occ_energy):
    ladder = ladder_of(amplitudes, integrals, screen_mask)
    residual = base_residual + ladder
    update = residual / (vir_energy[:, None] + occ_energy[None, :])
    return (residual, update)


def solution(mesh):
    in_specs = (
        P("row", "loop"),
        P("row", "loop"),
        P("row", None),
        P("row", "loop"),
        P("row"),
        P("loop"),
    )
    out_specs = (P("row", "loop"), P("row", "loop"))
    return jax.shard_map(
        on_device, mesh=mesh, in_specs=in_specs, out_specs=out_specs, check_vma=False
    )
```

time: 190 us -> 165 us (0.87)
  Pallas kernels: 185 us -> 161 us
    pallas_call x1, Pallas kernels: 185 us -> 161 us  [ladder_of(): pl.pallas_call(kernel, out_shape=jax.ShapeDtypeStruct((TILE, IC), F32), i...]
where the time goes in v2:
time: 165 us; the launch traced here: 163 us
  Pallas kernels  161 us (98%)
  other arithmetic  1.92 us (1%)
    pallas_call x1, Pallas kernels, ladder_of(): pl.pallas_call(kernel, out_shape=jax.ShapeDtypeStruct((TILE, IC), F32), i...  161 us

profile of v2, /device:TPU:100, one launch (start us, length us, event | category | flops | bytes accessed | tf_op | source)
XLA Modules:
  0.0 163.1 jit_solution(367446359828159944)
XLA Ops:
  0.6 0.0 copy-start.1
  0.6 0.0 copy-start.2
  0.7 0.0 copy-start
  0.7 160.5 %shard_map.77 = f32[128,768]{1,0:T(8,128)} custom-call(f32[2048,768]{1,0:T(8,128)} %amp_hbm.1, f32[2048,128]{1,0:T(8,128)} %int_hbm.1, s32[16,16]{1,0:T(8,128)} %mask.1), custom_call_target="tpu_custom_call" | custom-call | flops 19327352832 | bytes 25165824 | tf_op jit(solution)/shard_map/pallas_call | solution.py:426
  161.2 0.0 copy-done.1
  161.2 0.0 copy-done.2
  161.2 0.0 copy-done
  161.2 1.9 %add_divide_fusion = (f32[128,768]{1,0:T(8,128)}, f32[128,768]{1,0:T(8,128)}) fusion(f32[768]{0:T(1024)S(1)} %copy-done.1, f32[128]{0:T(128)S(1)} %copy-done.2, f32[128,768]{1,0:T(8,128)S(1)} %copy-done, f32[128,768]{1,0:T(8,128)} %shard_map.77), kind=kLoop, calls=%fused_computation | loop fusion | flops 294912 | bytes 1576448 | tf_op jit(solution)/shard_map/div | solution.py:473
Async XLA Ops:
  0.6 160.6 %copy-start.1 = (f32[768]{0:T(1024)S(1)}, f32[768]{0:T(1024)}, u32[]{:S(2)}) copy-start(f32[768]{0:T(1024)} %param.11) | copy-start | bytes 9220
  0.6 160.6 %copy-start.2 = (f32[128]{0:T(128)S(1)}, f32[128]{0:T(128)}, u32[]{:S(2)}) copy-start(f32[128]{0:T(128)} %param.10) | copy-start | bytes 1540
  0.7 160.6 %copy-start = (f32[128,768]{1,0:T(8,128)S(1)}, f32[128,768]{1,0:T(8,128)}, u32[]{:S(2)}) copy-start(f32[128,768]{1,0:T(8,128)} %param.9) | copy-start | bytes 1179652

commit v3 on v0

v3 whole, which is shorter than its diff:
```python
import jax
import jax.numpy as jnp
from jax import lax
from jax.experimental import pallas as pl
from jax.experimental.pallas import tpu as pltpu
from jax.sharding import PartitionSpec as P

TILE = 128
NL = 16
CR = 2048
HR = CR // 2
IC = 768
TI = 256
NT = IC // TI
BF = jnp.bfloat16
F32 = jnp.float32
MESH = pl.DeviceIdType.MESH

ORDER = [
    ("own",),
    ("prep",),
    ("block", 0, 0),
    ("own_second",),
    ("z_pass", 0, 1),
    ("z_pass", 0, 2),
    ("y_out", 0, 1),
    ("block", 1, 0),
    ("block", 2, 0),
    ("block", 0, 1),
    ("z_pass", 1, 1),
    ("z_pass", 1, 2),
    ("y_out", 1, 1),
    ("block", 3, 0),
    ("block", 1, 1),
    ("sum", 0, (0, 1), (0, 1), (0, 1, 2)),
    ("amp", 0),
    ("part", 0, 0, 0, 4),
    ("part", 1, 0, 0, 2),
    ("z_pass", 0, 3),
    ("y_out", 0, 2),
    ("block", 0, 2),
    ("block", 2, 1),
    ("z_pass", 1, 3),
    ("y_out", 1, 2),
    ("block", 1, 2),
    ("block", 3, 1),
    ("sum", 0, (2, 3), (0, 1), (0, 1, 2)),
    ("part", 1, 0, 2, 4),
    ("part", 2, 0, 0, 2),
    ("sum", 1, (0, 1, 2, 3), (0, 1), (0,)),
    ("amp", 1),
    ("y_out", 0, 3),
    ("part", 0, 1, 0, 4),
    ("part", 1, 1, 0, 4),
    ("part", 2, 1, 0, 2),
    ("block", 0, 3),
    ("block", 2, 2),
    ("sum", 1, (0, 1, 2, 3), (0, 1), (1,)),
    ("y_out", 1, 3),
    ("block", 1, 3),
    ("block", 3, 2),
    ("sum", 0, (0, 1), (2, 3), (0, 1, 2)),
    ("part", 2, 0, 2, 4),
    ("part", 2, 1, 2, 4),
    ("part", 3, 0, 0, 2),
    ("part", 3, 1, 0, 2),
    ("sum", 1, (0, 1), (2, 3), (0, 1)),
    ("amp", 2),
    ("part", 0, 2, 0, 4),
    ("part", 1, 2, 0, 4),
    ("sum", 1, (0, 1, 2, 3), (0, 1), (2,)),
    ("block", 2, 3),
    ("part", 2, 2, 0, 4),
    ("part", 3, 2, 0, 2),
    ("sum", 1, (0, 1), (2, 3), (2,)),
    ("part", 3, 0, 2, 3),
    ("part", 3, 1, 2, 3),
    ("part", 3, 2, 2, 3),
    ("total", 1, 0),
    ("sum", 1, (2,), (2, 3), (0, 1, 2)),
    ("sum", 0, (2,), (2, 3), (0, 1, 2)),
    ("sum", 1, (3,), (2,), (0, 1, 2)),
    ("sum", 0, (3,), (2,), (0, 1, 2)),
    ("total", 0, 0),
    ("last",),
    ("total", 1, 1),
    ("total", 0, 1),
]


def kernel(
    amp_hbm,
    int_hbm,
    mask,
    out,
    blk,
    t32,
    tp32,
    tth,
    ttl,
    rhs,
    pbuf,
    crecv,
    xrecv,
    srecv,
    zrecv,
    load_sem,
    g_recv,
    o_send,
    a_send,
    a_recv,
    y_send,
    z_send,
    zf_send,
    c_send,
    c_recv,
    x_send,
    x_recv,
    s_send,
    s_recv,
    h_send,
    h_recv,
):
    row = lax.axis_index("row")
    loop = lax.axis_index("loop")
    x, zh, core = row // 4, (row // 2) % 2, row % 2
    y, z = loop // 4, loop % 4
    half = y // 2
    zq = z // 2
    inner = ((z + 1) // 2) % 2 == 1
    zs = [z, z + 1 - 2 * (z % 2), 2 - zq, 3 - 3 * zq]

    def y_of(d):
        base = y + (d % 2) * (3 - 2 * y)
        return base + (d // 2) * (1 - 2 * (base % 2))

    def slot(d, k):
        return y_of(d) * 4 + zs[k]

    partner = (row, (3 - y) * 4 + z)
    ymate = (row, y_of(2) * 4 + z)
    znear = (row, y * 4 + zs[1])
    zfar = (row, y * 4 + 3 - z)
    mate = (row + 1 - 2 * core, loop)
    hpeer = (row + 2 - 4 * zh, loop)
    mine = pl.ds(pl.multiple_of(half * HR, HR), HR)
    theirs = pl.ds(pl.multiple_of((1 - half) * HR, HR), HR)

    barrier = pltpu.get_barrier_semaphore()
    peers = [partner, ymate, znear, mate, hpeer]
    peers += [(((x + j) % 4) * 4 + zh * 2 + core, loop) for j in (1, 2, 3)]
    for peer in peers:
        pl.semaphore_signal(barrier, inc=1, device_id=peer, device_id_type=MESH)

    @pl.when(inner)
    def _():
        pl.semaphore_signal(barrier, inc=1, device_id=zfar, device_id_type=MESH)

    load_b = pltpu.make_async_copy(int_hbm.at[mine], blk.at[loop], load_sem.at[1])
    load_b.start()
    load_t = pltpu.make_async_copy(amp_hbm.at[mine], t32, load_sem.at[0])
    load_t.start()
    pl.semaphore_wait(barrier, len(peers) + ((z + 1) // 2) % 2)

    def remote(src, dst, send, recv, to):
        return pltpu.make_async_remote_copy(
            src_ref=src,
            dst_ref=dst,
            send_sem=send,
            recv_sem=recv,
            device_id=to,
            device_id_type=MESH,
        )

    def tile(j):
        return pl.ds(j * TI, TI)

    def g_copy(d, k, send, to):
        s = slot(d, k)
        src = int_hbm.at[mine] if (d, k) == (0, 0) else blk.at[s]
        return remote(src, blk.at[s], send, g_recv.at[s], to)

    def half_copy():
        return remote(int_hbm.at[theirs], blk.at[loop], o_send, g_recv.at[loop], partner)

    def amp_copy(j):
        return remote(
            amp_hbm.at[theirs, tile(j)], tp32.at[j], a_send.at[j], a_recv.at[j], partner
        )

    def y_copy(d, k):
        return g_copy(d, k, y_send.at[d, k], ymate)

    def z_copy(d, far):
        return g_copy(d, 0, z_send.at[d, far], zfar if far else znear)

    def zf_copy(d, k):
        return g_copy(d, k, zf_send.at[d, k - 1], znear if k > 1 else zfar)

    def arrived(d, k):
        s = slot(d, k)
        remote(blk.at[s], blk.at[s], o_send, g_recv.at[s], partner).wait_recv()

    seen = {True: set(), False: set()}

    def need(d, k):
        if (d, k) == (0, 0):
            return
        todo = [where for where in seen if (d, k) not in seen[where]]
        for where in todo:
            seen[where].add((d, k))
        if len(todo) == 2:
            arrived(d, k)
        elif todo:

            @pl.when(inner if todo[0] else jnp.logical_not(inner))
            def _():
                arrived(d, k)

    def z_out(d):
        z_copy(d, 0).start()

        @pl.when(inner)
        def _():
            z_copy(d, 1).start()

    def own():
        half_copy().start()
        y_copy(0, 0).start()
        z_out(0)
        for j in range(NT):
            amp_copy(j).start()

    def own_second():
        need(1, 0)
        z_out(1)
        y_copy(1, 0).start()

    def z_pass(d, k):
        @pl.when(inner)
        def _():
            arrived(d, k)
            zf_copy(d, k).start()

        seen[True].add((d, k))

    def y_out(d, k):
        need(d, k)
        y_copy(d, k).start()

    def put_amp(q, rows, at, t):
        hi = t.astype(BF)
        tth[q, rows, pl.ds(at, 128)] = hi
        ttl[q, rows, pl.ds(at, 128)] = (t - hi.astype(F32)).astype(BF)

    def prep():
        load_t.wait()

        def body(i, carry):
            at = pl.multiple_of(i * 128, 128)
            put_amp(0, pl.ds(0, IC), at, t32[pl.ds(at, 128), :].T)
            return carry

        lax.fori_loop(0, HR // 128, body, 0)

    def amp(j):
        amp_copy(j).wait_recv()

        def body(i, carry):
            at = pl.multiple_of(i * 128, 128)
            put_amp(1, tile(j), at, tp32[j, pl.ds(at, 128), :].T)
            return carry

        lax.fori_loop(0, HR // 128, body, 0)

    def split(s):
        def body(i, carry):
            at = pl.multiple_of(i * 128, 128)
            m = blk[s, pl.ds(at, 128), :] * mask[half * (HR // 128) + i, s].astype(F32)
            hi = m.astype(BF)
            rhs[s, pl.ds(at, 128), 0:128] = hi
            rhs[s, pl.ds(at, 128), 128:256] = (m - hi.astype(F32)).astype(BF)
            return carry

        lax.fori_loop(0, HR // 128, body, 0)

    def multiply(q, s, j):
        at = pl.ds(pl.multiple_of(j * TI, TI), TI)
        a = jnp.dot(tth[q, at, :], rhs[s], preferred_element_type=F32)
        b = jnp.dot(ttl[q, at, :], rhs[s, :, 0:128], preferred_element_type=F32)
        pbuf[q, s, at, :] = a[:, 0:128] + (a[:, 128:256] + b)

    def keeps(k):
        return (zs[k] + core) % 2 == 0

    def c_copy(q, d, k, j):
        n = d * 2 + k // 2
        return remote(
            pbuf.at[q, slot(d, k), tile(j)],
            crecv.at[q, n, tile(j)],
            c_send.at[q, n, j],
            c_recv.at[q, n, j],
            mate,
        )

    def x_copy(q, d, p, s, j):
        yv = y_of(d)
        place = (x + 4 - yv) % 4 - 1
        to = (yv * 4 + zh * 2 + core, loop)
        return remote(
            pbuf.at[q, s, tile(j)],
            xrecv.at[q, place, p, tile(j)],
            x_send.at[q, d, p, j],
            x_recv.at[q, place, p, j],
            to,
        )

    def to_mate(q, d, k, j):
        @pl.when(jnp.logical_not(keeps(k)))
        def _():
            c_copy(q, d, k, j).start()

    def reduce(q, d, k, j):
        @pl.when(keeps(k))
        def _():
            n = d * 2 + k // 2
            s = slot(d, k)
            c_copy(q, d, k, j).wait_recv()
            pbuf[q, s, tile(j)] = pbuf[q, s, tile(j)] + crecv[q, n, tile(j)]

            @pl.when(x != y_of(d))
            def _():
                x_copy(q, d, k // 2, s, j).start()

    def ready(d, k):
        if (d, k) == (0, 0):
            load_b.wait()
        need(d, k)
        s = slot(d, k)
        split(s)
        return s

    def block(d, k):
        s = ready(d, k)

        def body(j, carry):
            multiply(0, s, j)
            return carry

        lax.fori_loop(0, NT, body, 0)
        for j in range(NT):
            to_mate(0, d, k, j)

    def part(k, j, low, high):
        def body(d, carry):
            multiply(1, slot(d, k), j)
            to_mate(1, d, k, j)
            return carry

        lax.fori_loop(low, high, body, 0)

    def sums(q, ds, ks, js):
        for d in ds:
            for k in ks:
                for j in js:
                    reduce(q, d, k, j)

    def last():
        s = ready(3, 3)
        todo = [(1, 0), (1, 1), (1, 2), (0, 0), (0, 1), (0, 2)]
        for n, (q, j) in enumerate(todo):
            multiply(q, s, j)
            to_mate(q, 3, 3, j)
            if n:
                reduce(todo[n - 1][0], 3, 3, todo[n - 1][1])
        reduce(0, 3, 3, NT - 1)

    def h_copy(s, j):
        return remote(
            pbuf.at[0, s, tile(j)], zrecv.at[tile(j)], h_send.at[j], h_recv.at[j], hpeer
        )

    def s_copy(p, s, j):
        return remote(
            pbuf.at[1, s, tile(j)],
            srecv.at[p, tile(j)],
            s_send.at[p, j],
            s_recv.at[p, j],
            partner,
        )

    def total(q, p):
        s = x * 4 + 2 * ((zq + p) % 2) + core
        for j in range(NT):
            for i in range(3):
                dst = xrecv.at[q, i, p, tile(j)]
                remote(dst, dst, o_send, x_recv.at[q, i, p, j], partner).wait_recv()
            add = (xrecv[q, 0, p, tile(j)] + xrecv[q, 1, p, tile(j)]) + xrecv[
                q, 2, p, tile(j)
            ]
            if q == 1:
                pbuf[1, s, tile(j)] = pbuf[1, s, tile(j)] + add
                s_copy(p, s, j).start()
            else:
                s_copy(p, s, j).wait_recv()
                pbuf[0, s, tile(j)] = (pbuf[0, s, tile(j)] + add) + srecv[p, tile(j)]

                @pl.when((zq + zh + p) % 2 == 1)
                def _():
                    h_copy(s, j).start()

    steps = {
        "own": own,
        "own_second": own_second,
        "z_pass": z_pass,
        "y_out": y_out,
        "prep": prep,
        "amp": amp,
        "block": block,
        "part": part,
        "last": last,
        "sum": sums,
        "total": total,
    }
    for name, *where in ORDER:
        steps[name](*where)
    s_mine = x * 4 + 2 * zh + core
    for j in range(NT):
        h_copy(s_mine, j).wait_recv()
        out[:, j * TI : (j + 1) * TI] = (pbuf[0, s_mine, tile(j)] + zrecv[tile(j)]).T

    sent = [half_copy(), z_copy(0, 0), z_copy(1, 0)]
    for j in range(NT):
        sent += [h_copy(s_mine, j), amp_copy(j)]
        sent += [s_copy(p, s_mine, j) for p in range(2)]
        sent += [c_copy(q, d, 2 * p, j) for q in (0, 1) for d in range(4) for p in (0, 1)]
    sent += [y_copy(d, k) for d in (0, 1) for k in range(4)]
    for c in sent:
        c.wait_send()

    @pl.when(inner)
    def _():
        for d in (0, 1):
            z_copy(d, 1).wait_send()
            for k in (1, 2, 3):
                zf_copy(d, k).wait_send()

    for d in range(4):

        @pl.when(x != y_of(d))
        def _():
            for q in (0, 1):
                for p in (0, 1):
                    for j in range(NT):
                        x_copy(q, d, p, loop, j).wait_send()


def ladder_of(amplitudes, integrals, screen_mask):
    dma = pltpu.SemaphoreType.DMA
    return pl.pallas_call(
        kernel,
        out_shape=jax.ShapeDtypeStruct((TILE, IC), F32),
        in_specs=[
            pl.BlockSpec(memory_space=pl.ANY),
            pl.BlockSpec(memory_space=pl.ANY),
            pl.BlockSpec(memory_space=pltpu.SMEM),
        ],
        out_specs=pl.BlockSpec(memory_space=pltpu.VMEM),
        scratch_shapes=[
            pltpu.VMEM((NL, HR, TILE), F32),
            pltpu.VMEM((HR, IC), F32),
            pltpu.VMEM((NT, HR, TI), F32),
            pltpu.VMEM((2, IC, HR), BF),
            pltpu.VMEM((2, IC, HR), BF),
            pltpu.VMEM((NL, HR, 2 * TILE), BF),
            pltpu.VMEM((2, NL, IC, TILE), F32),
            pltpu.VMEM((2, 8, IC, TILE), F32),
            pltpu.VMEM((2, 3, 2, IC, TILE), F32),
            pltpu.VMEM((2, IC, TILE), F32),
            pltpu.VMEM((IC, TILE), F32),
            dma((2,)),
            dma((NL,)),
            dma,
            dma((NT,)),
            dma((NT,)),
            dma((2, 4)),
            dma((2, 2)),
            dma((2, 3)),
            dma((2, 8, NT)),
            dma((2, 8, NT)),
            dma((2, 4, 2, NT)),
            dma((2, 3, 2, NT)),
            dma((2, NT)),
            dma((2, NT)),
            dma((NT,)),
            dma((NT,)),
        ],
        compiler_params=pltpu.CompilerParams(
            collective_id=0, has_side_effects=True, vmem_limit_bytes=60 * 1024 * 1024
        ),
        cost_estimate=pl.CostEstimate(
            flops=2 * 3 * CR * CR * IC, bytes_accessed=24 * 2**20, transcendentals=0
        ),
    )(amplitudes, integrals, screen_mask)


def on_device(amplitudes, integrals, screen_mask, base_residual, vir_energy, occ_energy):
    ladder = ladder_of(amplitudes, integrals, screen_mask)
    residual = base_residual + ladder
    update = residual / (vir_energy[:, None] + occ_energy[None, :])
    return (residual, update)


def solution(mesh):
    in_specs = (
        P("row", "loop"),
        P("row", "loop"),
        P("row", None),
        P("row", "loop"),
        P("row"),
        P("loop"),
    )
    out_specs = (P("row", "loop"), P("row", "loop"))
    return jax.shard_map(
        on_device, mesh=mesh, in_specs=in_specs, out_specs=out_specs, check_vma=False
    )
```

time: 550 us -> 165 us (0.30)
  waiting for transfers between devices: 472 us -> 0 us
  Pallas kernels: 0 us -> 162 us
  matrix products: 54.1 us -> 0 us
  between operations: 14.1 us -> 0.69 us
    all_gather x1 -> x0, waiting for transfers between devices: 354 us -> none  [on_device(): assembled = lax.all_gather(integrals, 'loop', axis=1, tiled=True)]
    pallas_call x0 -> x1, Pallas kernels: none -> 162 us  [ladder_of(): pl.pallas_call(kernel, out_shape=jax.ShapeDtypeStruct((TILE, IC), F32), i...]
    reduce_scatter x1 -> x0, waiting for transfers between devices: 118 us -> none  [on_device(): lax.psum_scatter(contract(screened, amplitudes), 'row', scatter_dimension...]
    dot_general x1 -> x0, matrix products: 54.1 us -> none  [contract(): lax.dot_general(panel, amplitudes, (((0,), (0,)), ((), ())), precision=la...]
  transfers between devices with their start and end apart: 2 -> 0, of which waited for: 2 -> 0; matrix products, arithmetic and copies ran while one was open for 0% -> 0% of each run, Pallas kernels for 0% -> 0%
where the time goes in v3:
time: 165 us
  Pallas kernels  162 us (98%)
  other arithmetic  1.92 us (1%)
    pallas_call x1, Pallas kernels, ladder_of(): pl.pallas_call(kernel, out_shape=jax.ShapeDtypeStruct((TILE, IC), F32), i...  162 us

profile of v3, /device:TPU:100, one launch (start us, length us, event | category | flops | bytes accessed | tf_op | source)
XLA Modules:
  0.0 164.7 jit_solution(329313894368921687)
XLA Ops:
  0.6 0.0 copy-start.1
  0.6 0.0 copy-start.2
  0.7 0.0 copy-start
  0.7 162.1 %shard_map.77 = f32[128,768]{1,0:T(8,128)} custom-call(f32[2048,768]{1,0:T(8,128)} %amp_hbm.1, f32[2048,128]{1,0:T(8,128)} %int_hbm.1, s32[16,16]{1,0:T(8,128)} %mask.1), custom_call_target="tpu_custom_call" | custom-call | flops 19327352832 | bytes 25165824 | tf_op jit(solution)/shard_map/pallas_call | solution.py:460
  162.8 0.0 copy-done.1
  162.8 0.0 copy-done.2
  162.8 0.0 copy-done
  162.8 1.9 %add_divide_fusion = (f32[128,768]{1,0:T(8,128)}, f32[128,768]{1,0:T(8,128)}) fusion(f32[768]{0:T(1024)S(1)} %copy-done.1, f32[128]{0:T(128)S(1)} %copy-done.2, f32[128,768]{1,0:T(8,128)S(1)} %copy-done, f32[128,768]{1,0:T(8,128)} %shard_map.77), kind=kLoop, calls=%fused_computation | loop fusion | flops 294912 | bytes 1576448 | tf_op jit(solution)/shard_map/div | solution.py:510
Async XLA Ops:
  0.6 162.2 %copy-start.1 = (f32[768]{0:T(1024)S(1)}, f32[768]{0:T(1024)}, u32[]{:S(2)}) copy-start(f32[768]{0:T(1024)} %param.11) | copy-start | bytes 9220
  0.6 162.2 %copy-start.2 = (f32[128]{0:T(128)S(1)}, f32[128]{0:T(128)}, u32[]{:S(2)}) copy-start(f32[128]{0:T(128)} %param.10) | copy-start | bytes 1540
  0.7 162.2 %copy-start = (f32[128,768]{1,0:T(8,128)S(1)}, f32[128,768]{1,0:T(8,128)}, u32[]{:S(2)}) copy-start(f32[128,768]{1,0:T(8,128)} %param.9) | copy-start | bytes 1179652

commit v4 on v3

--- a/solution.py
+++ b/solution.py
@@ -25,64 +25,83 @@
     ("z_pass", 0, 2),
     ("y_out", 0, 1),
     ("block", 1, 0),
+    ("sum", 0, (0,), (0,), (0, 1, 2)),
     ("block", 2, 0),
+    ("sum", 0, (1,), (0,), (0, 1, 2)),
     ("block", 0, 1),
+    ("sum", 0, (2,), (0,), (0, 1, 2)),
     ("z_pass", 1, 1),
     ("z_pass", 1, 2),
     ("y_out", 1, 1),
     ("block", 3, 0),
+    ("sum", 0, (0,), (1,), (0, 1, 2)),
     ("block", 1, 1),
-    ("sum", 0, (0, 1), (0, 1), (0, 1, 2)),
+    ("sum", 0, (3,), (0,), (0, 1, 2)),
+    ("sum", 0, (1,), (1,), (0, 1, 2)),
     ("amp", 0),
     ("part", 0, 0, 0, 4),
     ("part", 1, 0, 0, 2),
     ("z_pass", 0, 3),
     ("y_out", 0, 2),
+    ("sum", 1, (2, 3, 0, 1), (0,), (0,)),
+    ("sum", 1, (0, 1), (1,), (0,)),
     ("block", 0, 2),
     ("block", 2, 1),
+    ("sum", 0, (0,), (2,), (0, 1, 2)),
+    ("sum", 0, (2,), (1,), (0, 1, 2)),
     ("z_pass", 1, 3),
     ("y_out", 1, 2),
+    ("block", 3, 1),
     ("block", 1, 2),
-    ("block", 3, 1),
-    ("sum", 0, (2, 3), (0, 1), (0, 1, 2)),
+    ("sum", 0, (3,), (1,), (0, 1, 2)),
+    ("sum", 0, (1,), (2,), (0, 1, 2)),
     ("part", 1, 0, 2, 4),
     ("part", 2, 0, 0, 2),
-    ("sum", 1, (0, 1, 2, 3), (0, 1), (0,)),
+    ("sum", 1, (2, 3), (1,), (0,)),
+    ("sum", 1, (0, 1), (2,), (0,)),
     ("amp", 1),
     ("y_out", 0, 3),
     ("part", 0, 1, 0, 4),
     ("part", 1, 1, 0, 4),
-    ("part", 2, 1, 0, 2),
+    ("sum", 1, (2, 3, 0, 1), (0, 1), (1,)),
+    ("block", 2, 2),
     ("block", 0, 3),
-    ("block", 2, 2),
-    ("sum", 1, (0, 1, 2, 3), (0, 1), (1,)),
+    ("sum", 0, (2,), (2,), (0, 1, 2)),
+    ("sum", 0, (0,), (3,), (0, 1, 2)),
+    ("part", 2, 1, 0, 3),
+    ("part", 2, 0, 2, 3),
+    ("part", 3, 0, 0, 1),
+    ("part", 3, 1, 0, 1),
+    ("sum", 1, (2,), (2,), (0, 1)),
+    ("sum", 1, (0, 1), (2,), (1,)),
+    ("sum", 1, (0,), (3,), (0, 1)),
     ("y_out", 1, 3),
+    ("block", 3, 2),
     ("block", 1, 3),
-    ("block", 3, 2),
-    ("sum", 0, (0, 1), (2, 3), (0, 1, 2)),
-    ("part", 2, 0, 2, 4),
-    ("part", 2, 1, 2, 4),
-    ("part", 3, 0, 0, 2),
-    ("part", 3, 1, 0, 2),
-    ("sum", 1, (0, 1), (2, 3), (0, 1)),
+    ("sum", 0, (3,), (2,), (0, 1, 2)),
+    ("sum", 0, (1,), (3,), (0, 1, 2)),
+    ("part", 2, 0, 3, 4),
+    ("part", 2, 1, 3, 4),
+    ("sum", 1, (3,), (2,), (0, 1)),
+    ("part", 3, 0, 1, 2),
+    ("part", 3, 1, 1, 2),
+    ("sum", 1, (1,), (3,), (0, 1)),
     ("amp", 2),
     ("part", 0, 2, 0, 4),
     ("part", 1, 2, 0, 4),
-    ("sum", 1, (0, 1, 2, 3), (0, 1), (2,)),
+    ("sum", 1, (2, 3, 0, 1), (0, 1), (2,)),
     ("block", 2, 3),
     ("part", 2, 2, 0, 4),
-    ("part", 3, 2, 0, 2),
-    ("sum", 1, (0, 1), (2, 3), (2,)),
+    ("sum", 0, (2,), (3,), (0, 1, 2)),
+    ("sum", 1, (2, 3, 0, 1), (2,), (2,)),
+    ("part", 3, 2, 0, 3),
     ("part", 3, 0, 2, 3),
     ("part", 3, 1, 2, 3),
-    ("part", 3, 2, 2, 3),
+    ("sum", 1, (2,), (3,), (0, 1, 2)),
+    ("sum", 1, (0, 1), (3,), (2,)),
+    ("last",),
     ("total", 1, 0),
-    ("sum", 1, (2,), (2, 3), (0, 1, 2)),
-    ("sum", 0, (2,), (2, 3), (0, 1, 2)),
-    ("sum", 1, (3,), (2,), (0, 1, 2)),
-    ("sum", 0, (3,), (2,), (0, 1, 2)),
     ("total", 0, 0),
-    ("last",),
     ("total", 1, 1),
     ("total", 0, 1),
 ]

time: 165 us -> 147 us (0.89)
  the two profiles are of different devices: /device:TPU:100 before, /device:TPU:1 now
where the time goes in v4:
time: 147 us
  Pallas kernels  144 us (98%)
  other arithmetic  1.92 us (1%)
    pallas_call x1, Pallas kernels, ladder_of(): pl.pallas_call(kernel, out_shape=jax.ShapeDtypeStruct((TILE, IC), F32), i...  144 us

profile of v4, /device:TPU:1, one launch (start us, length us, event | category | flops | bytes accessed | tf_op | source)
XLA Modules:
  0.0 146.6 jit_solution(6502441403600571147)
XLA Ops:
  0.6 0.0 copy-start.1
  0.6 0.0 copy-start.2
  0.7 0.0 copy-start
  0.7 143.9 %shard_map.77 = f32[128,768]{1,0:T(8,128)} custom-call(f32[2048,768]{1,0:T(8,128)} %amp_hbm.1, f32[2048,128]{1,0:T(8,128)} %int_hbm.1, s32[16,16]{1,0:T(8,128)} %mask.1), custom_call_target="tpu_custom_call" | custom-call | flops 19327352832 | bytes 25165824 | tf_op jit(solution)/shard_map/pallas_call | solution.py:479
  144.6 0.0 copy-done.1
  144.6 0.0 copy-done.2
  144.6 0.0 copy-done
  144.6 1.9 %add_divide_fusion = (f32[128,768]{1,0:T(8,128)}, f32[128,768]{1,0:T(8,128)}) fusion(f32[768]{0:T(1024)S(1)} %copy-done.1, f32[128]{0:T(128)S(1)} %copy-done.2, f32[128,768]{1,0:T(8,128)S(1)} %copy-done, f32[128,768]{1,0:T(8,128)} %shard_map.77), kind=kLoop, calls=%fused_computation | loop fusion | flops 294912 | bytes 1576448 | tf_op jit(solution)/shard_map/div | solution.py:529
Async XLA Ops:
  0.6 144.0 %copy-start.1 = (f32[768]{0:T(1024)S(1)}, f32[768]{0:T(1024)}, u32[]{:S(2)}) copy-start(f32[768]{0:T(1024)} %param.11) | copy-start | bytes 9220
  0.6 144.0 %copy-start.2 = (f32[128]{0:T(128)S(1)}, f32[128]{0:T(128)}, u32[]{:S(2)}) copy-start(f32[128]{0:T(128)} %param.10) | copy-start | bytes 1540
  0.7 144.0 %copy-start = (f32[128,768]{1,0:T(8,128)S(1)}, f32[128,768]{1,0:T(8,128)}, u32[]{:S(2)}) copy-start(f32[128,768]{1,0:T(8,128)} %param.9) | copy-start | bytes 1179652

commit v5 on v4

--- a/solution.py
+++ b/solution.py
@@ -52,6 +52,7 @@
     ("z_pass", 1, 3),
     ("y_out", 1, 2),
     ("block", 3, 1),
+    ("z_more",),
     ("block", 1, 2),
     ("sum", 0, (3,), (1,), (0, 1, 2)),
     ("sum", 0, (1,), (2,), (0, 1, 2)),
@@ -64,6 +65,7 @@
     ("part", 0, 1, 0, 4),
     ("part", 1, 1, 0, 4),
     ("sum", 1, (2, 3, 0, 1), (0, 1), (1,)),
+    ("z_pass", 3, 3),
     ("block", 2, 2),
     ("block", 0, 3),
     ("sum", 0, (2,), (2,), (0, 1, 2)),
@@ -75,7 +77,6 @@
     ("sum", 1, (2,), (2,), (0, 1)),
     ("sum", 1, (0, 1), (2,), (1,)),
     ("sum", 1, (0,), (3,), (0, 1)),
-    ("y_out", 1, 3),
     ("block", 3, 2),
     ("block", 1, 3),
     ("sum", 0, (3,), (2,), (0, 1, 2)),
@@ -86,10 +87,12 @@
     ("part", 3, 0, 1, 2),
     ("part", 3, 1, 1, 2),
     ("sum", 1, (1,), (3,), (0, 1)),
+    ("total", 1, 0, (0, 1)),
     ("amp", 2),
     ("part", 0, 2, 0, 4),
     ("part", 1, 2, 0, 4),
     ("sum", 1, (2, 3, 0, 1), (0, 1), (2,)),
+    ("total", 0, 0, (0, 1)),
     ("block", 2, 3),
     ("part", 2, 2, 0, 4),
     ("sum", 0, (2,), (3,), (0, 1, 2)),
@@ -100,10 +103,10 @@
     ("sum", 1, (2,), (3,), (0, 1, 2)),
     ("sum", 1, (0, 1), (3,), (2,)),
     ("last",),
-    ("total", 1, 0),
-    ("total", 0, 0),
-    ("total", 1, 1),
-    ("total", 0, 1),
+    ("total", 1, 0, (2,)),
+    ("total", 0, 0, (2,)),
+    ("total", 1, 1, (0, 1, 2)),
+    ("total", 0, 1, (0, 1, 2)),
 ]
 
 
@@ -263,6 +266,11 @@
 
         seen[True].add((d, k))
 
+    def z_more():
+        @pl.when(inner)
+        def _():
+            zf_copy(3, 1).start()
+
     def y_out(d, k):
         need(d, k)
         y_copy(d, k).start()
@@ -408,9 +416,9 @@
             partner,
         )
 
-    def total(q, p):
+    def total(q, p, js):
         s = x * 4 + 2 * ((zq + p) % 2) + core
-        for j in range(NT):
+        for j in js:
             for i in range(3):
                 dst = xrecv.at[q, i, p, tile(j)]
                 remote(dst, dst, o_send, x_recv.at[q, i, p, j], partner).wait_recv()
@@ -432,6 +440,7 @@
         "own": own,
         "own_second": own_second,
         "z_pass": z_pass,
+        "z_more": z_more,
         "y_out": y_out,
         "prep": prep,
         "amp": amp,
@@ -453,7 +462,7 @@
         sent += [h_copy(s_mine, j), amp_copy(j)]
         sent += [s_copy(p, s_mine, j) for p in range(2)]
         sent += [c_copy(q, d, 2 * p, j) for q in (0, 1) for d in range(4) for p in (0, 1)]
-    sent += [y_copy(d, k) for d in (0, 1) for k in range(4)]
+    sent += [y_copy(d, k) for d in (0, 1) for k in range(4) if (d, k) != (1, 3)]
     for c in sent:
         c.wait_send()
 
@@ -463,6 +472,8 @@
             z_copy(d, 1).wait_send()
             for k in (1, 2, 3):
                 zf_copy(d, k).wait_send()
+        zf_copy(3, 1).wait_send()
+        zf_copy(3, 3).wait_send()
 
     for d in range(4):
 
@@ -504,7 +515,7 @@
             dma((NT,)),
             dma((2, 4)),
             dma((2, 2)),
-            dma((2, 3)),
+            dma((4, 3)),
             dma((2, 8, NT)),
             dma((2, 8, NT)),
             dma((2, 4, 2, NT)),

time: 147 us -> 141 us (0.959)
  the two profiles are of different devices: /device:TPU:1 before, /device:TPU:100 now
where the time goes in v5:
time: 141 us
  Pallas kernels  138 us (98%)
  other arithmetic  1.92 us (1%)
    pallas_call x1, Pallas kernels, ladder_of(): pl.pallas_call(kernel, out_shape=jax.ShapeDtypeStruct((TILE, IC), F32), i...  138 us

profile of v5, /device:TPU:100, one launch (start us, length us, event | category | flops | bytes accessed | tf_op | source)
XLA Modules:
  0.0 140.7 jit_solution(2385432809407689878)
XLA Ops:
  0.6 0.0 copy-start.1
  0.6 0.0 copy-start.2
  0.7 0.0 copy-start
  0.7 138.1 %shard_map.77 = f32[128,768]{1,0:T(8,128)} custom-call(f32[2048,768]{1,0:T(8,128)} %amp_hbm.1, f32[2048,128]{1,0:T(8,128)} %int_hbm.1, s32[16,16]{1,0:T(8,128)} %mask.1), custom_call_target="tpu_custom_call" | custom-call | flops 19327352832 | bytes 25165824 | tf_op jit(solution)/shard_map/pallas_call | solution.py:490
  138.8 0.0 copy-done.1
  138.8 0.0 copy-done.2
  138.8 0.0 copy-done
  138.8 1.9 %add_divide_fusion = (f32[128,768]{1,0:T(8,128)}, f32[128,768]{1,0:T(8,128)}) fusion(f32[768]{0:T(1024)S(1)} %copy-done.1, f32[128]{0:T(128)S(1)} %copy-done.2, f32[128,768]{1,0:T(8,128)S(1)} %copy-done, f32[128,768]{1,0:T(8,128)} %shard_map.77), kind=kLoop, calls=%fused_computation | loop fusion | flops 294912 | bytes 1576448 | tf_op jit(solution)/shard_map/div | solution.py:540
Async XLA Ops:
  0.6 138.1 %copy-start.1 = (f32[768]{0:T(1024)S(1)}, f32[768]{0:T(1024)}, u32[]{:S(2)}) copy-start(f32[768]{0:T(1024)} %param.11) | copy-start | bytes 9220
  0.6 138.1 %copy-start.2 = (f32[128]{0:T(128)S(1)}, f32[128]{0:T(128)}, u32[]{:S(2)}) copy-start(f32[128]{0:T(128)} %param.10) | copy-start | bytes 1540
  0.7 138.1 %copy-start = (f32[128,768]{1,0:T(8,128)S(1)}, f32[128,768]{1,0:T(8,128)}, u32[]{:S(2)}) copy-start(f32[128,768]{1,0:T(8,128)} %param.9) | copy-start | bytes 1179652

commit v6 on v5

--- a/solution.py
+++ b/solution.py
@@ -43,7 +43,7 @@
     ("part", 1, 0, 0, 2),
     ("z_pass", 0, 3),
     ("y_out", 0, 2),
-    ("sum", 1, (2, 3, 0, 1), (0,), (0,)),
+    ("sum", 1, (2, 0, 3, 1), (0,), (0,)),
     ("sum", 1, (0, 1), (1,), (0,)),
     ("block", 0, 2),
     ("block", 2, 1),
@@ -64,7 +64,7 @@
     ("y_out", 0, 3),
     ("part", 0, 1, 0, 4),
     ("part", 1, 1, 0, 4),
-    ("sum", 1, (2, 3, 0, 1), (0, 1), (1,)),
+    ("sum", 1, (2, 0, 3, 1), (0, 1), (1,)),
     ("z_pass", 3, 3),
     ("block", 2, 2),
     ("block", 0, 3),
@@ -91,12 +91,12 @@
     ("amp", 2),
     ("part", 0, 2, 0, 4),
     ("part", 1, 2, 0, 4),
-    ("sum", 1, (2, 3, 0, 1), (0, 1), (2,)),
+    ("sum", 1, (2, 0, 3, 1), (0, 1), (2,)),
     ("total", 0, 0, (0, 1)),
     ("block", 2, 3),
     ("part", 2, 2, 0, 4),
     ("sum", 0, (2,), (3,), (0, 1, 2)),
-    ("sum", 1, (2, 3, 0, 1), (2,), (2,)),
+    ("sum", 1, (2, 0, 3, 1), (2,), (2,)),
     ("part", 3, 2, 0, 3),
     ("part", 3, 0, 2, 3),
     ("part", 3, 1, 2, 3),
@@ -104,8 +104,8 @@
     ("sum", 1, (0, 1), (3,), (2,)),
     ("last",),
     ("total", 1, 0, (2,)),
+    ("total", 1, 1, (0, 1, 2)),
     ("total", 0, 0, (2,)),
-    ("total", 1, 1, (0, 1, 2)),
     ("total", 0, 1, (0, 1, 2)),
 ]
 
@@ -387,9 +387,9 @@
         lax.fori_loop(low, high, body, 0)
 
     def sums(q, ds, ks, js):
-        for d in ds:
-            for k in ks:
-                for j in js:
+        for k in ks:
+            for j in js:
+                for d in ds:
                     reduce(q, d, k, j)
 
     def last():
@@ -398,9 +398,10 @@
         for n, (q, j) in enumerate(todo):
             multiply(q, s, j)
             to_mate(q, 3, 3, j)
-            if n:
-                reduce(todo[n - 1][0], 3, 3, todo[n - 1][1])
-        reduce(0, 3, 3, NT - 1)
+            if n >= 3:
+                reduce(todo[n - 3][0], 3, 3, todo[n - 3][1])
+        for q, j in todo[3:]:
+            reduce(q, 3, 3, j)
 
     def h_copy(s, j):
         return remote(

time: 141 us -> 141 us (level)
  no operation moved by 1% of the time
where the time goes in v6:
time: 141 us; the launch traced here: 140 us
  Pallas kernels  138 us (98%)
  other arithmetic  1.92 us (1%)
    pallas_call x1, Pallas kernels, ladder_of(): pl.pallas_call(kernel, out_shape=jax.ShapeDtypeStruct((TILE, IC), F32), i...  138 us

profile of v6, /device:TPU:100, one launch (start us, length us, event | category | flops | bytes accessed | tf_op | source)
XLA Modules:
  0.0 140.2 jit_solution(7185396881399395219)
XLA Ops:
  0.6 0.0 copy-start.1
  0.6 0.0 copy-start.2
  0.7 0.0 copy-start
  0.7 137.6 %shard_map.77 = f32[128,768]{1,0:T(8,128)} custom-call(f32[2048,768]{1,0:T(8,128)} %amp_hbm.1, f32[2048,128]{1,0:T(8,128)} %int_hbm.1, s32[16,16]{1,0:T(8,128)} %mask.1), custom_call_target="tpu_custom_call" | custom-call | flops 19327352832 | bytes 25165824 | tf_op jit(solution)/shard_map/pallas_call | solution.py:491
  138.3 0.0 copy-done.1
  138.3 0.0 copy-done.2
  138.3 0.0 copy-done
  138.3 1.9 %add_divide_fusion = (f32[128,768]{1,0:T(8,128)}, f32[128,768]{1,0:T(8,128)}) fusion(f32[768]{0:T(1024)S(1)} %copy-done.1, f32[128]{0:T(128)S(1)} %copy-done.2, f32[128,768]{1,0:T(8,128)S(1)} %copy-done, f32[128,768]{1,0:T(8,128)} %shard_map.77), kind=kLoop, calls=%fused_computation | loop fusion | flops 294912 | bytes 1576448 | tf_op jit(solution)/shard_map/div | solution.py:541
Async XLA Ops:
  0.6 137.7 %copy-start.1 = (f32[768]{0:T(1024)S(1)}, f32[768]{0:T(1024)}, u32[]{:S(2)}) copy-start(f32[768]{0:T(1024)} %param.11) | copy-start | bytes 9220
  0.6 137.7 %copy-start.2 = (f32[128]{0:T(128)S(1)}, f32[128]{0:T(128)}, u32[]{:S(2)}) copy-start(f32[128]{0:T(128)} %param.10) | copy-start | bytes 1540
  0.7 137.7 %copy-start = (f32[128,768]{1,0:T(8,128)S(1)}, f32[128,768]{1,0:T(8,128)}, u32[]{:S(2)}) copy-start(f32[128,768]{1,0:T(8,128)} %param.9) | copy-start | bytes 1179652
